TPU v7x, 32 devices: a whole 2x2x4 slice. The times are simulated.
32 devices in a mesh: dp: 8 (over z, core), expert: 4 (over y, x).
Axes of the slice: x: 2, y: 2, z: 4, core: 2. Of those that a mesh axis runs over, the one named last changes fastest.
Arguments:
- tokens: bfloat16 [24576, 2048], P(('dp', 'expert')), may hold values from -6 to 6
- target: bfloat16 [24576, 2048], P(('dp', 'expert')), may hold values from -4 to 4
- route_index: int32 [8, 4, 4, 16], P('dp', None, 'expert'), may hold values from 0 to 767, as said below
- route_count: int32 [8, 4, 4], P('dp', None, 'expert'), may hold values from 1 to 16, as said below
- route_gate: float32 [8, 4, 4, 16], P('dp', None, 'expert'), may hold values from 0.1 to 1
- gate_weight: bfloat16 [2048, 4, 768], P('dp', 'expert'), may hold values from -0.125 to 0.125
- up_weight: bfloat16 [2048, 4, 768], P('dp', 'expert'), may hold values from -0.125 to 0.125
- down_weight: bfloat16 [2048, 4, 768], P('dp', 'expert'), may hold values from -0.21875 to 0.21875
Outputs:
- token_grad: bfloat16 [24576, 2048], P(('dp', 'expert'))
- gate_gradient: float32 [2048, 4, 768], P('dp', 'expert')
- up_gradient: float32 [2048, 4, 768], P('dp', 'expert')
- down_gradient: float32 [2048, 4, 768], P('dp', 'expert')
Inputs may be any that keep to these rules, and one draw needn't show every extreme that they name: `route_index`: within each list of 16 slots the indices are distinct; each names a token of the source device. `route_count`: in every group one expert has all 16 slots live from every source device; slots at or beyond the count are unused.
All inputs are finite; a program needn't handle non-finite values.
Results may differ from a plain program's by a relative error of at most 0.0059.
Values may be sent and summed in bfloat16 or wider, within the bound.
A program may use at most 128 MiB of HBM per device.

v0:
```python
import jax
import jax.numpy as jnp
from jax import lax
from jax.sharding import PartitionSpec as P


def to_owners(block):
    return lax.all_to_all(block, "expert", split_axis=0, concat_axis=1, tiled=True)


def to_sources(block):
    return lax.all_to_all(block, "expert", split_axis=1, concat_axis=0, tiled=True)


def on_device(
    tokens, target, route_index, route_count, route_gate, gate_weight, up_weight, down_weight
):
    groups = lax.axis_size("dp")
    sources = lax.axis_size("expert")
    local_index = route_index[0, :, 0, :]
    live_count = route_count[0, :, 0]
    per_source = local_index.shape[1]
    model_width = tokens.shape[1]
    usable = jnp.arange(per_source, dtype=jnp.int32)[None, :] < live_count[:, None]
    slot_weight = jnp.where(usable, route_gate[0, :, 0, :], 0.0)
    outgoing = tokens[local_index] * usable[:, :, None].astype(tokens.dtype)
    expert_rows = to_owners(outgoing)
    full_gate, full_up, full_down = (
        lax.all_gather(gate_weight, "dp", axis=0, tiled=True),
        lax.all_gather(up_weight, "dp", axis=0, tiled=True),
        lax.all_gather(down_weight, "dp", axis=0, tiled=True),
    )
    gate_pre = jnp.einsum(
        "erd,def->erf", expert_rows, full_gate, preferred_element_type=jnp.float32
    )
    up_pre = jnp.einsum("erd,def->erf", expert_rows, full_up, preferred_element_type=jnp.float32)
    sigma = jax.nn.sigmoid(gate_pre)
    active = gate_pre * sigma
    hidden = (active * up_pre).astype(jnp.bfloat16)
    expert_out = jnp.einsum(
        "erf,def->erd", hidden, full_down, preferred_element_type=jnp.float32
    ).astype(jnp.bfloat16)
    returned = to_sources(expert_out)
    flat_index = local_index.reshape(-1)
    combined = (
        jnp.zeros((tokens.shape[0], model_width), jnp.float32)
        .at[flat_index]
        .add((slot_weight[:, :, None] * returned.astype(jnp.float32)).reshape(-1, model_width))
    )
    out_grad = combined - target.astype(jnp.float32)
    slot_grad = (slot_weight[:, :, None] * out_grad[local_index]).astype(jnp.bfloat16)
    owner_grad = to_owners(slot_grad)
    hidden_grad = jnp.einsum(
        "erd,def->erf", owner_grad, full_down, preferred_element_type=jnp.float32
    )
    gate_grad = (hidden_grad * up_pre * sigma * (1.0 + gate_pre * (1.0 - sigma))).astype(
        jnp.bfloat16
    )
    up_grad = (hidden_grad * active).astype(jnp.bfloat16)
    row_grad = (
        jnp.einsum("erf,def->erd", gate_grad, full_gate, preferred_element_type=jnp.float32)
        + jnp.einsum("erf,def->erd", up_grad, full_up, preferred_element_type=jnp.float32)
    ).astype(jnp.bfloat16)
    came_back = to_sources(row_grad)
    token_grad = (
        jnp.zeros((tokens.shape[0], model_width), jnp.float32)
        .at[flat_index]
        .add(came_back.astype(jnp.float32).reshape(-1, model_width))
        .astype(jnp.bfloat16)
    )
    factor = (groups * sources * per_source) ** (-0.5)
    rows_every, grad_every = (
        lax.all_to_all(expert_rows, "dp", split_axis=2, concat_axis=1, tiled=True),
        lax.all_to_all(owner_grad, "dp", split_axis=2, concat_axis=1, tiled=True),
    )
    hidden_piece = lax.all_gather(hidden, "dp", axis=1, tiled=True)
    gate_piece = lax.all_gather(gate_grad, "dp", axis=1, tiled=True)
    up_piece = lax.all_gather(up_grad, "dp", axis=1, tiled=True)
    gate_sum = jnp.einsum(
        "erd,erf->def", rows_every, gate_piece, preferred_element_type=jnp.float32
    )
    up_sum = jnp.einsum("erd,erf->def", rows_every, up_piece, preferred_element_type=jnp.float32)
    down_sum = jnp.einsum(
        "erd,erf->def", grad_every, hidden_piece, preferred_element_type=jnp.float32
    )
    gate_gradient = gate_sum * factor
    up_gradient = up_sum * factor
    down_gradient = down_sum * factor
    return (token_grad, gate_gradient, up_gradient, down_gradient)


def solution(mesh):
    return jax.shard_map(
        on_device,
        mesh=mesh,
        in_specs=(
            P(("dp", "expert"), None),
            P(("dp", "expert"), None),
            P("dp", None, "expert", None),
            P("dp", None, "expert"),
            P("dp", None, "expert", None),
            P("dp", "expert", None),
            P("dp", "expert", None),
            P("dp", "expert", None),
        ),
        out_specs=(
            P(("dp", "expert"), None),
            P("dp", "expert", None),
            P("dp", "expert", None),
            P("dp", "expert", None),
        ),
        check_vma=False,
    )
```

profile of v0, /device:TPU:0, one launch (start us, length us, event | category | flops | bytes accessed | tf_op | source)
XLA Modules:
  0.0 305.2 jit_solution(9919206521907058066)
XLA Ops:
  11.8 5.2 %all-to-all-start = ((bf16[4,16,2048]{2,1,0:T(8,128)(2,1)}), bf16[4,16,2048]{2,1,0:T(8,128)(2,1)S(1)}, u32[]{:S(2)}, u32[]{:S(2)}) async-start(bf16[4,16,2048]{2,1,0:T(8,128)(2,1)} %broadcast_multiply_fusion), calls=%async_computation | async-start | bytes 524288 | tf_op jit(solution)/shard_map/all_to_all | solution.py:8
  18.3 4.1 %all-to-all-done = bf16[4,16,2048]{2,1,0:T(8,128)(2,1)S(1)} async-done(((bf16[4,16,2048]{2,1,0:T(8,128)(2,1)}), bf16[4,16,2048]{2,1,0:T(8,128)(2,1)S(1)}, u32[]{:S(2)}, u32[]{:S(2)}) %all-to-all-start) | async-done | bytes 262176 | tf_op jit(solution)/shard_map/all_to_all | solution.py:8
  24.9 13.3 %reduce.10 = bf16[2048,64]{1,0:T(8,128)(2,1)} reduce(bf16[2048,1,64]{2,1,0:T(2,128)(2,1)} %bitcast.114, bf16[]{:T(256)} %broadcast.134), dimensions={1}, to_apply=%bitcast.86.reduce_sub_computation | reduce | bytes 524290
  40.3 4.9 %all-to-all-start.4 = ((bf16[8,2,8192]{2,1,0:T(2,128)(2,1)}), bf16[8,2,8192]{2,1,0:T(2,128)(2,1)}, u32[]{:S(2)}, u32[]{:S(2)}) async-start(bf16[8,2,8192]{2,1,0:T(2,128)(2,1)} %reshape.301), calls=%async_computation.4 | async-start | bytes 524288 | tf_op jit(solution)/shard_map/all_to_all | solution.py:73
  46.6 8.4 %all-to-all-done.4 = bf16[8,2,8192]{2,1,0:T(2,128)(2,1)} async-done(((bf16[8,2,8192]{2,1,0:T(2,128)(2,1)}), bf16[8,2,8192]{2,1,0:T(2,128)(2,1)}, u32[]{:S(2)}, u32[]{:S(2)}) %all-to-all-start.4) | async-done | bytes 262176 | tf_op jit(solution)/shard_map/all_to_all | solution.py:73
  58.4 3.4 %copy.41 = bf16[1,64,2048]{2,1,0:T(8,128)(2,1)} copy(bf16[1,64,2048]{1,0,2:T(2,128)(2,1)} %bitcast.112) | data formatting | bytes 524288 | tf_op jit(solution)/shard_map/all_to_all | solution.py:73
  66.8 24.2 %all-gather.9.cloned.1.call-done = bf16[2048,1,768]{2,0,1:T(8,128)(2,1)} async-done(((bf16[256,1,768]{2,0,1:T(8,128)(2,1)}), bf16[2048,1,768]{2,0,1:T(8,128)(2,1)}) %all-gather.9.cloned.1.call-update) | async-done | bytes 3145744 | tf_op jit(solution)/shard_map/all_gather | solution.py:30
  94.1 35.6 %all-gather.11.cloned.1.call-done = bf16[2048,1,768]{2,0,1:T(8,128)(2,1)} async-done(((bf16[256,1,768]{2,0,1:T(8,128)(2,1)}), bf16[2048,1,768]{2,0,1:T(8,128)(2,1)}) %all-gather.11.cloned.1.call-update) | async-done | bytes 3145744 | tf_op jit(solution)/shard_map/all_gather | solution.py:31
  133.9 3.8 %reduce.8 = bf16[64,2048]{1,0:T(8,128)(2,1)} reduce(bf16[64,1,2048]{2,1,0:T(2,128)(2,1)} %bitcast.123, bf16[]{:T(256)} %broadcast.134), dimensions={1}, to_apply=%bitcast.109.reduce_sub_computation | reduce | bytes 524290
  139.5 4.2 %all-to-all-start.1 = ((bf16[4,2,16384]{2,1,0:T(2,128)(2,1)}), bf16[4,2,16384]{2,1,0:T(2,128)(2,1)}, u32[]{:S(2)}, u32[]{:S(2)}) async-start(bf16[4,2,16384]{2,1,0:T(2,128)(2,1)} %reshape.297), calls=%async_computation.1 | async-start | bytes 524288 | tf_op jit(solution)/shard_map/all_to_all | solution.py:12
  143.8 5.8 %all-to-all-done.1 = bf16[4,2,16384]{2,1,0:T(2,128)(2,1)} async-done(((bf16[4,2,16384]{2,1,0:T(2,128)(2,1)}), bf16[4,2,16384]{2,1,0:T(2,128)(2,1)}, u32[]{:S(2)}, u32[]{:S(2)}) %all-to-all-start.1) | async-done | bytes 262176 | tf_op jit(solution)/shard_map/all_to_all | solution.py:12
  151.5 5.1 %scatter_custom_fusion = f32[768,2048]{1,0:T(8,128)} fusion(s32[64]{0:T(128)S(1)} %fusion.41, f32[]{:T(128)} %constant.5.clone.1, bf16[1,64,2048]{2,0,1:T(2,128)(2,1)} %bitcast.122, f32[64]{0:T(128)S(1)} %broadcast_select_fusion.1), kind=kCustom, calls=%fused_computation.19 | custom fusion | flops 393216 | bytes 6554116 | tf_op jit(solution)/shard_map/scatter-add | solution.py:48
  156.6 7.9 %convert_subtract_fusion = f32[768,2048]{1,0:T(8,128)} fusion(f32[768,2048]{1,0:T(8,128)} %scatter_custom_fusion, bf16[768,2048]{1,0:T(8,128)(2,1)} %param.9), kind=kLoop, calls=%fused_computation.4 | loop fusion | flops 3145728 | bytes 15728640 | tf_op jit(solution)/shard_map/sub | solution.py:50
  164.4 4.6 %gather_fusion.1 = f32[64,2048]{1,0:T(8,128)} fusion(f32[768,2048]{1,0:T(8,128)} %convert_subtract_fusion, s32[1024]{0:T(1024)S(1)} %pad_clamp_fusion), kind=kCustom, calls=%fused_computation.1 | custom fusion | bytes 1048832 | tf_op jit(solution)/shard_map/gather | solution.py:51
  170.8 4.1 %all-to-all-start.2 = ((bf16[4,16,2048]{2,1,0:T(8,128)(2,1)}), bf16[4,16,2048]{2,1,0:T(8,128)(2,1)}, u32[]{:S(2)}, u32[]{:S(2)}) async-start(bf16[4,16,2048]{2,1,0:T(8,128)(2,1)} %multiply_convert_fusion), calls=%async_computation.2 | async-start | bytes 524288 | tf_op jit(solution)/shard_map/all_to_all | solution.py:8
  174.9 16.5 %all-gather.2 = bf16[512,768]{1,0:T(8,128)(2,1)} all-gather(bf16[64,768]{1,0:T(8,128)(2,1)S(1)} %get-tuple-element.28), channel_id=4, replica_groups=mesh['dp'=8,'expert'=4] {'dp'}, dimensions={0}, use_global_device_ids=true | all-gather | bytes 884736 | tf_op jit(solution)/shard_map/all_gather | solution.py:76
  197.7 3.8 %reduce.9 = bf16[64,2048]{1,0:T(8,128)(2,1)} reduce(bf16[64,1,2048]{2,1,0:T(2,128)(2,1)} %bitcast.124, bf16[]{:T(256)} %broadcast.134), dimensions={1}, to_apply=%bitcast.108.reduce_sub_computation | reduce | bytes 524290
  203.4 4.2 %all-to-all-start.3 = ((bf16[4,2,16384]{2,1,0:T(2,128)(2,1)}), bf16[4,2,16384]{2,1,0:T(2,128)(2,1)}, u32[]{:S(2)}, u32[]{:S(2)}) async-start(bf16[4,2,16384]{2,1,0:T(2,128)(2,1)} %reshape.299), calls=%async_computation.3 | async-start | bytes 524288 | tf_op jit(solution)/shard_map/all_to_all | solution.py:12
  207.6 16.5 %all-gather = bf16[512,768]{1,0:T(8,128)(2,1)S(1)} all-gather(bf16[64,768]{1,0:T(8,128)(2,1)} %copy-done.4), channel_id=2, replica_groups=mesh['dp'=8,'expert'=4] {'dp'}, dimensions={0}, use_global_device_ids=true | all-gather | bytes 884736 | tf_op jit(solution)/shard_map/all_gather | solution.py:77
  231.8 13.3 %reduce.11 = bf16[2048,64]{1,0:T(8,128)(2,1)} reduce(bf16[2048,1,64]{2,1,0:T(2,128)(2,1)} %bitcast.115, bf16[]{:T(256)} %broadcast.134), dimensions={1}, to_apply=%bitcast.88.reduce_sub_computation | reduce | bytes 524290
  247.3 4.1 %all-to-all-start.5 = ((bf16[8,2,8192]{2,1,0:T(2,128)(2,1)}), bf16[8,2,8192]{2,1,0:T(2,128)(2,1)}, u32[]{:S(2)}, u32[]{:S(2)}) async-start(bf16[8,2,8192]{2,1,0:T(2,128)(2,1)} %reshape.303), calls=%async_computation.5 | async-start | bytes 524288 | tf_op jit(solution)/shard_map/all_to_all | solution.py:74
  251.3 19.9 %all-gather.1 = bf16[512,768]{1,0:T(8,128)(2,1)S(1)} all-gather(bf16[64,768]{1,0:T(8,128)(2,1)S(1)} %get-tuple-element.25), channel_id=3, replica_groups=mesh['dp'=8,'expert'=4] {'dp'}, dimensions={0}, use_global_device_ids=true | all-gather | bytes 884736 | tf_op jit(solution)/shard_map/all_gather | solution.py:78
  277.5 5.1 %scatter_custom_fusion.1 = f32[768,2048]{1,0:T(8,128)} fusion(s32[64]{0:T(128)S(1)} %fusion.41, f32[]{:T(128)} %constant.5.clone.1, bf16[1,64,2048]{2,0,1:T(2,128)(2,1)} %bitcast.125), kind=kCustom, calls=%fused_computation.17 | custom fusion | flops 262144 | bytes 6553604 | tf_op jit(solution)/shard_map/scatter-add | solution.py:68
  282.5 4.9 %convert_element_type.75 = bf16[768,2048]{1,0:T(8,128)(2,1)} convert(f32[768,2048]{1,0:T(8,128)} %scatter_custom_fusion.1) | non-fusion elementwise | flops 1572864 | bytes 9437184 | tf_op jit(solution)/shard_map/convert_element_type | solution.py:69
  (75 shorter events, 68.6 us)
Async XLA Ops:
  7.2 3.0 copy-start
  7.2 10.4 %copy-start.5 = (s32[1,4,1,16]{3,2,1,0:T(1,128)S(1)}, s32[1,4,1,16]{3,2,1,0:T(1,128)}, u32[]{:S(2)}) copy-start(s32[1,4,1,16]{3,2,1,0:T(1,128)} %param.10) | copy-start | bytes 772
  7.2 3.8 %copy-start.7 = (s32[1,4,1]{1,2,0:T(1,128)S(1)}, s32[1,4,1]{1,2,0:T(1,128)}, u32[]{:S(2)}) copy-start(s32[1,4,1]{1,2,0:T(1,128)} %param.11) | copy-start | bytes 52
  7.2 56.3 %all-gather.7.cloned.1.call-start = ((), (), s32[]{:S(2)}) async-start(), calls=%async_computation.6 | async-start | bytes 3538944 | tf_op jit(solution)/shard_map/all_gather | solution.py:29
  7.9 83.0 %all-gather.9.cloned.1.call-start = ((), (), s32[]{:S(2)}) async-start(), calls=%async_computation.7 | async-start | bytes 3538944 | tf_op jit(solution)/shard_map/all_gather | solution.py:30
  8.7 121.0 %all-gather.11.cloned.1.call-start = ((), (), s32[]{:S(2)}) async-start(), calls=%async_computation.8 | async-start | bytes 3538944 | tf_op jit(solution)/shard_map/all_gather | solution.py:31
  10.9 34.9 %copy-start.6 = (f32[1,4,1,16]{3,2,1,0:T(1,128)S(1)}, f32[1,4,1,16]{3,2,1,0:T(1,128)}, u32[]{:S(2)}) copy-start(f32[1,4,1,16]{3,2,1,0:T(1,128)} %param.12) | copy-start | bytes 772
  11.8 10.6 %all-to-all-start = ((bf16[4,16,2048]{2,1,0:T(8,128)(2,1)}), bf16[4,16,2048]{2,1,0:T(8,128)(2,1)S(1)}, u32[]{:S(2)}, u32[]{:S(2)}) async-start(bf16[4,16,2048]{2,1,0:T(8,128)(2,1)} %broadcast_multiply_fusion), calls=%async_computation | async-start | bytes 524288 | tf_op jit(solution)/shard_map/all_to_all | solution.py:8
  40.3 14.7 %all-to-all-start.4 = ((bf16[8,2,8192]{2,1,0:T(2,128)(2,1)}), bf16[8,2,8192]{2,1,0:T(2,128)(2,1)}, u32[]{:S(2)}, u32[]{:S(2)}) async-start(bf16[8,2,8192]{2,1,0:T(2,128)(2,1)} %reshape.301), calls=%async_computation.4 | async-start | bytes 524288 | tf_op jit(solution)/shard_map/all_to_all | solution.py:73
  94.1 49.6 %copy-start.3 = (bf16[8,8,8,256]{3,2,1,0:T(8,128)(2,1)S(1)}, bf16[8,8,8,256]{3,2,1,0:T(8,128)(2,1)}, u32[]{:S(2)}) copy-start(bf16[8,8,8,256]{3,2,1,0:T(8,128)(2,1)} %copy.49) | copy-start | bytes 786436
  139.5 10.2 %all-to-all-start.1 = ((bf16[4,2,16384]{2,1,0:T(2,128)(2,1)}), bf16[4,2,16384]{2,1,0:T(2,128)(2,1)}, u32[]{:S(2)}, u32[]{:S(2)}) async-start(bf16[4,2,16384]{2,1,0:T(2,128)(2,1)} %reshape.297), calls=%async_computation.1 | async-start | bytes 524288 | tf_op jit(solution)/shard_map/all_to_all | solution.py:12
  170.8 20.5 %all-to-all-start.2 = ((bf16[4,16,2048]{2,1,0:T(8,128)(2,1)}), bf16[4,16,2048]{2,1,0:T(8,128)(2,1)}, u32[]{:S(2)}, u32[]{:S(2)}) async-start(bf16[4,16,2048]{2,1,0:T(8,128)(2,1)} %multiply_convert_fusion), calls=%async_computation.2 | async-start | bytes 524288 | tf_op jit(solution)/shard_map/all_to_all | solution.py:8
  191.4 3.0 copy-start.2
  191.4 4.1 %copy-start.1 = (bf16[2048,1,768]{2,0,1:T(8,128)(2,1)S(1)}, bf16[2048,1,768]{2,0,1:T(8,128)(2,1)}, u32[]{:S(2)}) copy-start(bf16[2048,1,768]{2,0,1:T(8,128)(2,1)} %all-gather.7.cloned.1.call-done) | copy-start | bytes 9437188
  194.2 2.3 copy-start.4
  203.4 43.9 %all-to-all-start.3 = ((bf16[4,2,16384]{2,1,0:T(2,128)(2,1)}), bf16[4,2,16384]{2,1,0:T(2,128)(2,1)}, u32[]{:S(2)}, u32[]{:S(2)}) async-start(bf16[4,2,16384]{2,1,0:T(2,128)(2,1)} %reshape.299), calls=%async_computation.3 | async-start | bytes 524288 | tf_op jit(solution)/shard_map/all_to_all | solution.py:12
  247.3 40.2 %all-to-all-start.5 = ((bf16[8,2,8192]{2,1,0:T(2,128)(2,1)}), bf16[8,2,8192]{2,1,0:T(2,128)(2,1)}, u32[]{:S(2)}, u32[]{:S(2)}) async-start(bf16[8,2,8192]{2,1,0:T(2,128)(2,1)} %reshape.303), calls=%async_computation.5 | async-start | bytes 524288 | tf_op jit(solution)/shard_map/all_to_all | solution.py:74
Sparse Core Ops, SparseCore 0:
  9.6 40.9 all-gather.6
  52.3 38.6 all-gather.8
  92.6 37.1 all-gather.10
where the time goes:
time: 307 us; the launch traced here: 305 us
  waiting for transfers between devices  80.1 us (26%)
  other arithmetic  62 us (20%)
  blocking collectives  52.9 us (17%)
  local copies, waits for them, and re-layouts  50.3 us (16%)
  starting transfers between devices  26.7 us (9%)
  matrix products  19.3 us (6%)
  between operations  13.9 us (5%)
    all_gather x1, waiting for transfers between devices, on_device(): lax.all_gather(down_weight, 'dp', axis=0, tiled=True)  35.6 us
    unnamed x6, other arithmetic  35.6 us
    unnamed x32, local copies, waits for them, and re-layouts  31.1 us
    all_gather x1, waiting for transfers between devices, on_device(): lax.all_gather(up_weight, 'dp', axis=0, tiled=True)  24.2 us
    all_gather x1, blocking collectives, on_device(): up_piece = lax.all_gather(up_grad, 'dp', axis=1, tiled=True)  19.9 us
    all_gather x1, blocking collectives, on_device(): gate_piece = lax.all_gather(gate_grad, 'dp', axis=1, tiled=True)  16.5 us
    all_gather x1, blocking collectives, on_device(): hidden_piece = lax.all_gather(hidden, 'dp', axis=1, tiled=True)  16.5 us
    all_to_all x2, starting transfers between devices, to_owners(): lax.all_to_all(block, 'expert', split_axis=0, concat_axis=1, tiled=True)  9.24 us
  transfers between devices with their start and end apart: 9, of which 5 were waited for; matrix products, arithmetic and copies ran while one was open for 25% of the time, Pallas kernels for 0%

commit v1 on v0

--- a/solution.py
+++ b/solution.py
@@ -75,7 +75,12 @@
     )
     hidden_piece = lax.all_gather(hidden, "dp", axis=1, tiled=True)
     gate_piece = lax.all_gather(gate_grad, "dp", axis=1, tiled=True)
-    up_piece = lax.all_gather(up_grad, "dp", axis=1, tiled=True)
+    ring = [up_grad]
+    for hop in range(7):
+        ring.append(lax.ppermute(ring[-1], "dp", [(dev, (dev + 1) % 8) for dev in range(8)]))
+    up_piece = jnp.roll(
+        jnp.concatenate(ring[::-1], axis=1), (lax.axis_index("dp") + 1) * ring[0].shape[1], axis=1
+    )
     gate_sum = jnp.einsum(
         "erd,erf->def", rows_every, gate_piece, preferred_element_type=jnp.float32
     )

time: 307 us -> 326 us (1.062)
  waiting for transfers between devices: 80.1 us -> 102 us
  blocking collectives: 52.9 us -> 37.6 us
  local copies, waits for them, and re-layouts: 50.3 us -> 63.1 us
    all_gather x1 -> x0, blocking collectives: 19.9 us -> none  [on_device(): up_piece = lax.all_gather(up_grad, 'dp', axis=1, tiled=True)]
    all_gather x1, waiting for transfers between devices: 24.2 us -> 37.2 us  [on_device(): lax.all_gather(up_weight, 'dp', axis=0, tiled=True)]
    ppermute x0 -> x7, waiting for transfers between devices: none -> 12.7 us  [on_device(): lax.ppermute(ring[-1], 'dp', [(dev, (dev + 1) % 8) for dev in range(8)])]
    unnamed x32 -> x51, local copies, waits for them, and re-layouts: 31.1 us -> 42.7 us
    all_to_all x1, waiting for transfers between devices: 8.38 us -> 0.01 us  [on_device(): lax.all_to_all(expert_rows, 'dp', split_axis=2, concat_axis=1, tiled=True)]
    all_to_all x2, waiting for transfers between devices: 5.82 us -> 0.01 us  [to_sources(): lax.all_to_all(block, 'expert', split_axis=1, concat_axis=0, tiled=True)]
    all_gather x1, waiting for transfers between devices: 0.01 us -> 5.51 us  [on_device(): lax.all_gather(gate_weight, 'dp', axis=0, tiled=True)]
    all_to_all x2, waiting for transfers between devices: 4.11 us -> 8.51 us  [to_owners(): lax.all_to_all(block, 'expert', split_axis=0, concat_axis=1, tiled=True)]
  transfers between devices with their start and end apart: 9 -> 16, of which waited for: 5 -> 8; matrix products, arithmetic and copies ran while one was open for 25% -> 32% of each run, Pallas kernels for 0% -> 0%
where the time goes in v1:
time: 326 us; the launch traced here: 323 us
  waiting for transfers between devices  102 us (31%)
  local copies, waits for them, and re-layouts  63.1 us (19%)
  other arithmetic  61 us (19%)
  blocking collectives  37.6 us (12%)
  starting transfers between devices  27.6 us (8%)
  matrix products  18.2 us (6%)
  between operations  14 us (4%)
    unnamed x51, local copies, waits for them, and re-layouts  42.7 us
    all_gather x1, waiting for transfers between devices, on_device(): lax.all_gather(up_weight, 'dp', axis=0, tiled=True)  37.2 us
    all_gather x1, waiting for transfers between devices, on_device(): lax.all_gather(down_weight, 'dp', axis=0, tiled=True)  35.6 us
    unnamed x6, other arithmetic  34.6 us
    all_gather x1, blocking collectives, on_device(): gate_piece = lax.all_gather(gate_grad, 'dp', axis=1, tiled=True)  20 us
    all_gather x1, blocking collectives, on_device(): hidden_piece = lax.all_gather(hidden, 'dp', axis=1, tiled=True)  17.6 us
    ppermute x7, waiting for transfers between devices, on_device(): lax.ppermute(ring[-1], 'dp', [(dev, (dev + 1) % 8) for dev in range(8)])  12.7 us
    all_to_all x2, starting transfers between devices, to_owners(): lax.all_to_all(block, 'expert', split_axis=0, concat_axis=1, tiled=True)  9.38 us
  transfers between devices with their start and end apart: 16, of which 8 were waited for; matrix products, arithmetic and copies ran while one was open for 32% of the time, Pallas kernels for 0%

profile of v1, /device:TPU:0, one launch (start us, length us, event | category | flops | bytes accessed | tf_op | source)
XLA Modules:
  0.0 323.1 jit_solution(6411702034247937369)
XLA Ops:
  11.8 5.2 %all-to-all-start = ((bf16[4,16,2048]{2,1,0:T(8,128)(2,1)}), bf16[4,16,2048]{2,1,0:T(8,128)(2,1)S(1)}, u32[]{:S(2)}, u32[]{:S(2)}) async-start(bf16[4,16,2048]{2,1,0:T(8,128)(2,1)} %broadcast_multiply_fusion), calls=%async_computation | async-start | bytes 524288 | tf_op jit(solution)/shard_map/all_to_all | solution.py:8
  24.8 13.3 %reduce.10 = bf16[2048,64]{1,0:T(8,128)(2,1)} reduce(bf16[2048,1,64]{2,1,0:T(2,128)(2,1)} %bitcast.119, bf16[]{:T(256)} %broadcast.135), dimensions={1}, to_apply=%bitcast.92.reduce_sub_computation | reduce | bytes 524290
  40.2 4.9 %all-to-all-start.4 = ((bf16[8,2,8192]{2,1,0:T(2,128)(2,1)}), bf16[8,2,8192]{2,1,0:T(2,128)(2,1)}, u32[]{:S(2)}, u32[]{:S(2)}) async-start(bf16[8,2,8192]{2,1,0:T(2,128)(2,1)} %reshape.299), calls=%async_computation.4 | async-start | bytes 524288 | tf_op jit(solution)/shard_map/all_to_all | solution.py:73
  45.1 5.5 %all-gather.6.cloned.1.call-done = bf16[2048,1,768]{2,0,1:T(8,128)(2,1)} async-done(((bf16[256,1,768]{2,0,1:T(8,128)(2,1)}), bf16[2048,1,768]{2,0,1:T(8,128)(2,1)}) %all-gather.6.cloned.1.call-update) | async-done | bytes 3145744 | tf_op jit(solution)/shard_map/all_gather | solution.py:29
  53.8 37.2 %all-gather.8.cloned.1.call-done = bf16[2048,1,768]{2,0,1:T(8,128)(2,1)} async-done(((bf16[256,1,768]{2,0,1:T(8,128)(2,1)}), bf16[2048,1,768]{2,0,1:T(8,128)(2,1)}) %all-gather.8.cloned.1.call-update) | async-done | bytes 3145744 | tf_op jit(solution)/shard_map/all_gather | solution.py:30
  94.2 35.6 %all-gather.10.cloned.1.call-done = bf16[2048,1,768]{2,0,1:T(8,128)(2,1)} async-done(((bf16[256,1,768]{2,0,1:T(8,128)(2,1)}), bf16[2048,1,768]{2,0,1:T(8,128)(2,1)}) %all-gather.10.cloned.1.call-update) | async-done | bytes 3145744 | tf_op jit(solution)/shard_map/all_gather | solution.py:31
  137.9 3.6 %all-to-all-start.1 = ((bf16[4,2,16384]{2,1,0:T(2,128)(2,1)}), bf16[4,2,16384]{2,1,0:T(2,128)(2,1)S(1)}, u32[]{:S(2)}, u32[]{:S(2)}) async-start(bf16[4,2,16384]{2,1,0:T(2,128)(2,1)} %reshape.295), calls=%async_computation.1 | async-start | bytes 524288 | tf_op jit(solution)/shard_map/all_to_all | solution.py:12
  145.0 3.4 %copy.41 = bf16[1,64,2048]{2,1,0:T(8,128)(2,1)} copy(bf16[1,64,2048]{1,0,2:T(2,128)(2,1)} %bitcast.117) | data formatting | bytes 524288 | tf_op jit(solution)/shard_map/all_to_all | solution.py:73
  151.0 5.1 %scatter_custom_fusion = f32[768,2048]{1,0:T(8,128)} fusion(s32[64]{0:T(128)S(1)} %fusion.43, f32[]{:T(128)} %constant.15.clone.1, bf16[1,64,2048]{2,0,1:T(2,128)(2,1)} %bitcast.127, f32[64]{0:T(128)S(1)} %broadcast_select_fusion.1), kind=kCustom, calls=%fused_computation.19 | custom fusion | flops 393216 | bytes 6554116 | tf_op jit(solution)/shard_map/scatter-add | solution.py:48
  156.1 7.8 %convert_subtract_fusion = f32[768,2048]{1,0:T(8,128)} fusion(f32[768,2048]{1,0:T(8,128)} %scatter_custom_fusion, bf16[768,2048]{1,0:T(8,128)(2,1)} %param.9), kind=kLoop, calls=%fused_computation.4 | loop fusion | flops 3145728 | bytes 15728640 | tf_op jit(solution)/shard_map/sub | solution.py:50
  163.9 4.6 %gather_fusion.1 = f32[64,2048]{1,0:T(8,128)} fusion(f32[768,2048]{1,0:T(8,128)} %convert_subtract_fusion, s32[1024]{0:T(1024)S(1)} %pad_clamp_fusion), kind=kCustom, calls=%fused_computation.1 | custom fusion | bytes 1048832 | tf_op jit(solution)/shard_map/gather | solution.py:51
  170.4 4.2 %all-to-all-start.2 = ((bf16[4,16,2048]{2,1,0:T(8,128)(2,1)}), bf16[4,16,2048]{2,1,0:T(8,128)(2,1)}, u32[]{:S(2)}, u32[]{:S(2)}) async-start(bf16[4,16,2048]{2,1,0:T(8,128)(2,1)} %multiply_convert_fusion), calls=%async_computation.2 | async-start | bytes 524288 | tf_op jit(solution)/shard_map/all_to_all | solution.py:8
  174.6 5.8 %all-to-all-done.2 = bf16[4,16,2048]{2,1,0:T(8,128)(2,1)} async-done(((bf16[4,16,2048]{2,1,0:T(8,128)(2,1)}), bf16[4,16,2048]{2,1,0:T(8,128)(2,1)}, u32[]{:S(2)}, u32[]{:S(2)}) %all-to-all-start.2) | async-done | bytes 262176 | tf_op jit(solution)/shard_map/all_to_all | solution.py:8
  184.6 4.8 %collective-permute-done = bf16[1,64,768]{2,1,0:T(8,128)(2,1)} collective-permute-done((bf16[1,64,768]{2,1,0:T(8,128)(2,1)S(1)}, bf16[1,64,768]{2,1,0:T(8,128)(2,1)}, u32[]{:S(2)}, u32[]{:S(2)}) %collective-permute-start) | collective-permute-done | bytes 98336 | tf_op jit(solution)/shard_map/ppermute | solution.py:80
  191.6 3.7 %reduce.9 = bf16[64,2048]{1,0:T(8,128)(2,1)} reduce(bf16[64,1,2048]{2,1,0:T(2,128)(2,1)} %bitcast.129, bf16[]{:T(256)} %broadcast.135), dimensions={1}, to_apply=%bitcast.113.reduce_sub_computation | reduce | bytes 524290
  197.2 4.0 %all-to-all-start.3 = ((bf16[4,2,16384]{2,1,0:T(2,128)(2,1)}), bf16[4,2,16384]{2,1,0:T(2,128)(2,1)}, u32[]{:S(2)}, u32[]{:S(2)}) async-start(bf16[4,2,16384]{2,1,0:T(2,128)(2,1)} %reshape.297), calls=%async_computation.3 | async-start | bytes 524288 | tf_op jit(solution)/shard_map/all_to_all | solution.py:12
  201.3 17.6 %all-gather.1 = bf16[512,768]{1,0:T(8,128)(2,1)} all-gather(bf16[64,768]{1,0:T(8,128)(2,1)} %copy-done.5), channel_id=3, replica_groups=mesh['dp'=8,'expert'=4] {'dp'}, dimensions={0}, use_global_device_ids=true | all-gather | bytes 884736 | tf_op jit(solution)/shard_map/all_gather | solution.py:76
  218.9 3.4 %copy.43 = bf16[1,64,2048]{1,0,2:T(2,128)(2,1)} copy(bf16[1,64,2048]{2,1,0:T(8,128)(2,1)} %bitcast.24) | data formatting | bytes 524288 | tf_op jit(solution)/shard_map/all_to_all | solution.py:8
  222.3 13.3 %reduce.11 = bf16[2048,64]{1,0:T(8,128)(2,1)} reduce(bf16[2048,1,64]{2,1,0:T(2,128)(2,1)} %bitcast.120, bf16[]{:T(256)} %broadcast.135), dimensions={1}, to_apply=%bitcast.94.reduce_sub_computation | reduce | bytes 524290
  238.0 4.7 %all-to-all-start.5 = ((bf16[8,2,8192]{2,1,0:T(2,128)(2,1)}), bf16[8,2,8192]{2,1,0:T(2,128)(2,1)}, u32[]{:S(2)}, u32[]{:S(2)}) async-start(bf16[8,2,8192]{2,1,0:T(2,128)(2,1)} %reshape.301), calls=%async_computation.5 | async-start | bytes 524288 | tf_op jit(solution)/shard_map/all_to_all | solution.py:74
  242.8 20.0 %all-gather = bf16[512,768]{1,0:T(8,128)(2,1)S(1)} all-gather(bf16[64,768]{1,0:T(8,128)(2,1)} %copy-done.6), channel_id=2, replica_groups=mesh['dp'=8,'expert'=4] {'dp'}, dimensions={0}, use_global_device_ids=true | all-gather | bytes 884736 | tf_op jit(solution)/shard_map/all_gather | solution.py:77
  269.3 5.1 %scatter_custom_fusion.1 = f32[768,2048]{1,0:T(8,128)} fusion(s32[64]{0:T(128)S(1)} %fusion.43, f32[]{:T(128)} %constant.15.clone.1, bf16[1,64,2048]{2,0,1:T(2,128)(2,1)} %bitcast.130), kind=kCustom, calls=%fused_computation.17 | custom fusion | flops 262144 | bytes 6553604 | tf_op jit(solution)/shard_map/scatter-add | solution.py:68
  274.4 4.9 %convert_element_type.75 = bf16[768,2048]{1,0:T(8,128)(2,1)} convert(f32[768,2048]{1,0:T(8,128)} %scatter_custom_fusion.1) | non-fusion elementwise | flops 1572864 | bytes 9437184 | tf_op jit(solution)/shard_map/convert_element_type | solution.py:69
  287.4 6.1 %collective-permute-done.5 = bf16[1,64,768]{2,1,0:T(8,128)(2,1)} collective-permute-done((bf16[1,64,768]{2,1,0:T(8,128)(2,1)}, bf16[1,64,768]{2,1,0:T(8,128)(2,1)}, u32[]{:S(2)}, u32[]{:S(2)}) %collective-permute-start.5) | collective-permute-done | bytes 98336 | tf_op jit(solution)/shard_map/ppermute | solution.py:80
  (108 shorter events, 85.3 us)
Async XLA Ops:
  7.2 43.4 %all-gather.6.cloned.1.call-start = ((), (), s32[]{:S(2)}) async-start(), calls=%async_computation.6 | async-start | bytes 3538944 | tf_op jit(solution)/shard_map/all_gather | solution.py:29
  7.9 3.0 copy-start.9
  7.9 83.1 %all-gather.8.cloned.1.call-start = ((), (), s32[]{:S(2)}) async-start(), calls=%async_computation.7 | async-start | bytes 3538944 | tf_op jit(solution)/shard_map/all_gather | solution.py:30
  8.7 121.2 %all-gather.10.cloned.1.call-start = ((), (), s32[]{:S(2)}) async-start(), calls=%async_computation.8 | async-start | bytes 3538944 | tf_op jit(solution)/shard_map/all_gather | solution.py:31
  10.2 7.3 %copy-start.7 = (s32[1,4,1,16]{3,2,1,0:T(1,128)S(1)}, s32[1,4,1,16]{3,2,1,0:T(1,128)}, u32[]{:S(2)}) copy-start(s32[1,4,1,16]{3,2,1,0:T(1,128)} %param.10) | copy-start | bytes 772
  10.2 8.7 %copy-start.8 = (f32[1,4,1,16]{3,2,1,0:T(1,128)S(1)}, f32[1,4,1,16]{3,2,1,0:T(1,128)}, u32[]{:S(2)}) copy-start(f32[1,4,1,16]{3,2,1,0:T(1,128)} %param.12) | copy-start | bytes 772
  11.8 10.6 %all-to-all-start = ((bf16[4,16,2048]{2,1,0:T(8,128)(2,1)}), bf16[4,16,2048]{2,1,0:T(8,128)(2,1)S(1)}, u32[]{:S(2)}, u32[]{:S(2)}) async-start(bf16[4,16,2048]{2,1,0:T(8,128)(2,1)} %broadcast_multiply_fusion), calls=%async_computation | async-start | bytes 524288 | tf_op jit(solution)/shard_map/all_to_all | solution.py:8
  40.2 97.7 %all-to-all-start.4 = ((bf16[8,2,8192]{2,1,0:T(2,128)(2,1)}), bf16[8,2,8192]{2,1,0:T(2,128)(2,1)}, u32[]{:S(2)}, u32[]{:S(2)}) async-start(bf16[8,2,8192]{2,1,0:T(2,128)(2,1)} %reshape.299), calls=%async_computation.4 | async-start | bytes 524288 | tf_op jit(solution)/shard_map/all_to_all | solution.py:73
  94.2 38.6 %copy-start.5 = (bf16[64,768]{1,0:T(8,128)(2,1)}, bf16[64,768]{1,0:T(8,128)(2,1)S(1)}, u32[]{:S(2)}) copy-start(bf16[64,768]{1,0:T(8,128)(2,1)S(1)} %get-tuple-element.28) | copy-start | bytes 294916
  137.9 12.1 %all-to-all-start.1 = ((bf16[4,2,16384]{2,1,0:T(2,128)(2,1)}), bf16[4,2,16384]{2,1,0:T(2,128)(2,1)S(1)}, u32[]{:S(2)}, u32[]{:S(2)}) async-start(bf16[4,2,16384]{2,1,0:T(2,128)(2,1)} %reshape.295), calls=%async_computation.1 | async-start | bytes 524288 | tf_op jit(solution)/shard_map/all_to_all | solution.py:12
  163.9 10.6 %copy-start.4 = (bf16[8,8,8,256]{3,2,1,0:T(8,128)(2,1)S(1)}, bf16[8,8,8,256]{3,2,1,0:T(8,128)(2,1)}, u32[]{:S(2)}) copy-start(bf16[8,8,8,256]{3,2,1,0:T(8,128)(2,1)} %copy.49) | copy-start | bytes 786436
  170.4 10.1 %all-to-all-start.2 = ((bf16[4,16,2048]{2,1,0:T(8,128)(2,1)}), bf16[4,16,2048]{2,1,0:T(8,128)(2,1)}, u32[]{:S(2)}, u32[]{:S(2)}) async-start(bf16[4,16,2048]{2,1,0:T(8,128)(2,1)} %multiply_convert_fusion), calls=%async_computation.2 | async-start | bytes 524288 | tf_op jit(solution)/shard_map/all_to_all | solution.py:8
  183.3 6.0 %copy-start.6 = (bf16[64,768]{1,0:T(8,128)(2,1)}, bf16[64,768]{1,0:T(8,128)(2,1)S(1)}, u32[]{:S(2)}) copy-start(bf16[64,768]{1,0:T(8,128)(2,1)S(1)} %get-tuple-element.24) | copy-start | bytes 294916
  183.3 6.0 %copy-start.1 = (bf16[2048,1,768]{2,0,1:T(8,128)(2,1)S(1)}, bf16[2048,1,768]{2,0,1:T(8,128)(2,1)}, u32[]{:S(2)}) copy-start(bf16[2048,1,768]{2,0,1:T(8,128)(2,1)} %all-gather.6.cloned.1.call-done) | copy-start | bytes 9437188
  183.3 6.0 %collective-permute-start = (bf16[1,64,768]{2,1,0:T(8,128)(2,1)S(1)}, bf16[1,64,768]{2,1,0:T(8,128)(2,1)}, u32[]{:S(2)}, u32[]{:S(2)}) collective-permute-start(bf16[1,64,768]{2,1,0:T(8,128)(2,1)S(1)} %bitcast.131), channel_id=1, source_target_pairs={{0,4},{4,8},{8,12},{12,16},{16,20},{20,24},{24,28},{28,0},{1,5},{5... | collective-permute-start | bytes 294920 | tf_op jit(solution)/shard_map/ppermute | solution.py:80
  189.3 11.9 %collective-permute-start.1 = (bf16[1,64,768]{2,1,0:T(8,128)(2,1)}, bf16[1,64,768]{2,1,0:T(8,128)(2,1)}, u32[]{:S(2)}, u32[]{:S(2)}) collective-permute-start(bf16[1,64,768]{2,1,0:T(8,128)(2,1)} %collective-permute-done), channel_id=1, source_target_pairs={{0,4},{4,8},{8,12},{12,16},{16,20},{20,24},{24,28},{28,0},{1,5},{5... | collective-permute-start | bytes 294920 | tf_op jit(solution)/shard_map/ppermute | solution.py:80
  197.2 40.9 %all-to-all-start.3 = ((bf16[4,2,16384]{2,1,0:T(2,128)(2,1)}), bf16[4,2,16384]{2,1,0:T(2,128)(2,1)}, u32[]{:S(2)}, u32[]{:S(2)}) async-start(bf16[4,2,16384]{2,1,0:T(2,128)(2,1)} %reshape.297), calls=%async_computation.3 | async-start | bytes 524288 | tf_op jit(solution)/shard_map/all_to_all | solution.py:12
  201.2 36.5 %collective-permute-start.2 = (bf16[1,64,768]{2,1,0:T(8,128)(2,1)}, bf16[1,64,768]{2,1,0:T(8,128)(2,1)}, u32[]{:S(2)}, u32[]{:S(2)}) collective-permute-start(bf16[1,64,768]{2,1,0:T(8,128)(2,1)} %collective-permute-done.1), channel_id=1, source_target_pairs={{0,4},{4,8},{8,12},{12,16},{16,20},{20,24},{24,28},{28,0},{1,5},{5... | collective-permute-start | bytes 294920 | tf_op jit(solution)/shard_map/ppermute | solution.py:80
  237.7 25.1 %collective-permute-start.3 = (bf16[1,64,768]{2,1,0:T(8,128)(2,1)}, bf16[1,64,768]{2,1,0:T(8,128)(2,1)}, u32[]{:S(2)}, u32[]{:S(2)}) collective-permute-start(bf16[1,64,768]{2,1,0:T(8,128)(2,1)} %collective-permute-done.2), channel_id=1, source_target_pairs={{0,4},{4,8},{8,12},{12,16},{16,20},{20,24},{24,28},{28,0},{1,5},{5... | collective-permute-start | bytes 294920 | tf_op jit(solution)/shard_map/ppermute | solution.py:80
  238.0 41.3 %all-to-all-start.5 = ((bf16[8,2,8192]{2,1,0:T(2,128)(2,1)}), bf16[8,2,8192]{2,1,0:T(2,128)(2,1)}, u32[]{:S(2)}, u32[]{:S(2)}) async-start(bf16[8,2,8192]{2,1,0:T(2,128)(2,1)} %reshape.301), calls=%async_computation.5 | async-start | bytes 524288 | tf_op jit(solution)/shard_map/all_to_all | solution.py:74
  262.8 24.4 %collective-permute-start.4 = (bf16[1,64,768]{2,1,0:T(8,128)(2,1)}, bf16[1,64,768]{2,1,0:T(8,128)(2,1)}, u32[]{:S(2)}, u32[]{:S(2)}) collective-permute-start(bf16[1,64,768]{2,1,0:T(8,128)(2,1)} %collective-permute-done.3), channel_id=1, source_target_pairs={{0,4},{4,8},{8,12},{12,16},{16,20},{20,24},{24,28},{28,0},{1,5},{5... | collective-permute-start | bytes 294920 | tf_op jit(solution)/shard_map/ppermute | solution.py:80
  286.1 7.3 %copy-start.3 = (bf16[512,768]{1,0:T(8,128)(2,1)S(1)}, bf16[512,768]{1,0:T(8,128)(2,1)}, u32[]{:S(2)}) copy-start(bf16[512,768]{1,0:T(8,128)(2,1)} %all-gather.1) | copy-start | bytes 2359300
  287.2 6.2 %collective-permute-start.5 = (bf16[1,64,768]{2,1,0:T(8,128)(2,1)}, bf16[1,64,768]{2,1,0:T(8,128)(2,1)}, u32[]{:S(2)}, u32[]{:S(2)}) collective-permute-start(bf16[1,64,768]{2,1,0:T(8,128)(2,1)} %collective-permute-done.4), channel_id=1, source_target_pairs={{0,4},{4,8},{8,12},{12,16},{16,20},{20,24},{24,28},{28,0},{1,5},{5... | collective-permute-start | bytes 294920 | tf_op jit(solution)/shard_map/ppermute | solution.py:80
  293.4 6.2 %collective-permute-start.6 = (bf16[1,64,768]{2,1,0:T(8,128)(2,1)}, bf16[1,64,768]{2,1,0:T(8,128)(2,1)}, u32[]{:S(2)}, u32[]{:S(2)}) collective-permute-start(bf16[1,64,768]{2,1,0:T(8,128)(2,1)} %collective-permute-done.5), channel_id=1, source_target_pairs={{0,4},{4,8},{8,12},{12,16},{16,20},{20,24},{24,28},{28,0},{1,5},{5... | collective-permute-start | bytes 294920 | tf_op jit(solution)/shard_map/ppermute | solution.py:80
  (2 other events, 6.1 us)
Sparse Core Ops, SparseCore 0:
  9.6 40.9 all-gather.5
  52.2 38.7 all-gather.7
  92.7 37.1 all-gather.9
